TPU v7x, 32 devices: a whole 2x2x4 slice. The times are simulated.
32 devices in a mesh: seq: 2 (over core), grp: 16 (over z, y, x).
Axes of the slice: x: 2, y: 2, z: 4, core: 2. Of those that a mesh axis runs over, the one named last changes fastest.
Arguments:
- inputs: bfloat16 [2, 16, 1024, 768], P(None, 'grp', 'seq'), may hold values from -6 to 6
- cotangent: bfloat16 [2, 16, 1024, 768], P(None, 'grp', 'seq'), may hold values from -6 to 6
- query_weight: bfloat16 [768, 768], P(('seq', 'grp')), may hold values from -0.3125 to 0.3125
- query_bias: bfloat16 [768], P(('seq', 'grp')), may hold values from -1.5 to 1.5
- key_weight: bfloat16 [768, 768], P(('seq', 'grp')), may hold values from -0.3125 to 0.3125
- value_weight: bfloat16 [768, 768], P(('seq', 'grp')), may hold values from -0.21875 to 0.21875
- value_bias: bfloat16 [768], P(('seq', 'grp')), may hold values from -1.5 to 1.5
- output_weight: bfloat16 [768, 768], P(('seq', 'grp')), may hold values from -1.25 to 1.25
- output_bias: bfloat16 [768], P(('seq', 'grp')), may hold values from -1.5 to 1.5
- first_gain: bfloat16 [768], P(('seq', 'grp')), may hold values from 0.5 to 1.5
- first_shift: bfloat16 [768], P(('seq', 'grp')), may hold values from -1.5 to 1.5
- inner_weight: bfloat16 [768, 3072], P(('seq', 'grp')), may hold values from -0.21875 to 0.21875
- inner_bias: bfloat16 [3072], P(('seq', 'grp')), may hold values from -1.5 to 1.5
- outer_weight: bfloat16 [3072, 768], P(('seq', 'grp')), may hold values from -0.109375 to 0.109375
- outer_bias: bfloat16 [768], P(('seq', 'grp')), may hold values from -1.5 to 1.5
- second_gain: bfloat16 [768], P(('seq', 'grp')), may hold values from 0.5 to 1.5
- second_shift: bfloat16 [768], P(('seq', 'grp')), may hold values from -1.5 to 1.5
Outputs:
- layer_out: bfloat16 [2, 16, 1024, 768], P(None, 'grp', 'seq')
- input_gradient: bfloat16 [2, 16, 1024, 768], P(None, 'grp', 'seq')
- query_weight_gradient: float32 [768, 768], P(('seq', 'grp'))
- query_bias_gradient: float32 [768], P(('seq', 'grp'))
- key_weight_gradient: float32 [768, 768], P(('seq', 'grp'))
- value_weight_gradient: float32 [768, 768], P(('seq', 'grp'))
- value_bias_gradient: float32 [768], P(('seq', 'grp'))
- output_weight_gradient: float32 [768, 768], P(('seq', 'grp'))
- output_bias_gradient: float32 [768], P(('seq', 'grp'))
- first_gain_gradient: float32 [768], P(('seq', 'grp'))
- first_shift_gradient: float32 [768], P(('seq', 'grp'))
- inner_weight_gradient: float32 [768, 3072], P(('seq', 'grp'))
- inner_bias_gradient: float32 [3072], P(('seq', 'grp'))
- outer_weight_gradient: float32 [3072, 768], P(('seq', 'grp'))
- outer_bias_gradient: float32 [768], P(('seq', 'grp'))
- second_gain_gradient: float32 [768], P(('seq', 'grp'))
- second_shift_gradient: float32 [768], P(('seq', 'grp'))
All inputs are finite; a program needn't handle non-finite values.
Results may differ from a plain program's by a relative error of at most 0.015.
The roundings to bfloat16 on the way count: a program that leaves them out, or rounds other values in their place, can miss the bound.
Values may be sent and summed in bfloat16 or wider, within the bound.
A program may use at most 192 MiB of HBM per device.

v0:
```python
import functools

import jax
import jax.numpy as jnp
from jax import lax
from jax.experimental import pallas as pl
from jax.experimental.pallas import tpu as pltpu
from jax.sharding import PartitionSpec as P

HEADS = 12
SCALE = 0.125
EPS = 1e-05
PAIR = 128
ROWS = 256
CHUNK = 768
LANES = 128
GROUP = 256
LAG = 3
AHEAD = 4
VMEM_LIMIT = 64 * 1024 * 1024 - 65536
GELU_C = 0.7978845608028654
GELU_A = 0.044715
MESH = pl.DeviceIdType.MESH
F32 = jnp.float32
BF16 = jnp.bfloat16


def dot_nn(left, right):
    return lax.dot_general(left, right, (((1,), (0,)), ((), ())), preferred_element_type=F32)


def dot_nt(left, right):
    return lax.dot_general(left, right, (((1,), (1,)), ((), ())), preferred_element_type=F32)


def dot_tn(left, right):
    return lax.dot_general(left, right, (((0,), (0,)), ((), ())), preferred_element_type=F32)


def place():
    s = lax.axis_index("seq")
    g = lax.axis_index("grp")
    return s, g // 4, (g // 2) % 2, g % 2


def device(s, z, y, x):
    return (s, z * 4 + y * 2 + x)


def first_partner(s, z, y, x):
    return device(s, z, y * s + (1 - y) * (1 - s), x * (1 - s) + (1 - x) * s)


def second_partner(s, z, y, x):
    return device(s, z, y * (1 - s) + (1 - y) * s, x * s + (1 - x) * (1 - s))


def greet(s, z, y, x):
    barrier = pltpu.get_barrier_semaphore()
    partners = [device(1 - s, z, y, x), first_partner(s, z, y, x), second_partner(s, z, y, x)]
    partners += [device(s, (z + k) % 4, y, x) for k in (1, 2, 3)]
    for partner in partners:
        pl.semaphore_signal(barrier, inc=1, device_id=partner, device_id_type=MESH)
    pl.semaphore_wait(barrier, len(partners))


def remote(src, dst, send, recv, target):
    return pltpu.make_async_remote_copy(
        src_ref=src, dst_ref=dst, send_sem=send, recv_sem=recv, device_id=target, device_id_type=MESH
    )


def selector(lanes, width, piece):
    lane = lax.broadcasted_iota(jnp.int32, (lanes, width), 0)
    col = lax.broadcasted_iota(jnp.int32, (lanes, width), 1)
    return (lax.rem(col, piece) == lane).astype(BF16)


def owned(devices, rows, width, piece):
    dev = lax.broadcasted_iota(jnp.int32, (devices, rows, width), 0)
    col = lax.broadcasted_iota(jnp.int32, (devices, rows, width), 2)
    return col // piece == dev


def spread(pieces, width):
    devices, rows, lanes = pieces.shape
    piece = width // devices
    flat = pieces.reshape(devices * rows, lanes).astype(BF16)
    tiled = dot_nn(flat, selector(lanes, width, piece)).reshape(devices, rows, width)
    return jnp.sum(jnp.where(owned(devices, rows, width, piece), tiled, 0.0), axis=0)


def collect(values, devices):
    rows, width = values.shape
    piece = width // devices
    mine = jnp.where(owned(devices, rows, width, piece), values[None], 0.0)
    flat = mine.reshape(devices * rows, width).astype(BF16)
    return dot_nt(flat, selector(LANES, width, piece)).reshape(devices, rows, LANES)


class Gather:
    def __init__(self, shards, fulls, own_sem, send, recv, chunks, where):
        self.shards, self.fulls, self.chunks, self.where = shards, fulls, chunks, where
        self.own_sem, self.send, self.recv = own_sem, send, recv

    def piece(self, i):
        a, r, nr, c, nc = self.chunks[i]
        return self.shards[a].at[r : r + nr, c : c + nc]

    def full(self, i, *where):
        a, r, nr, c, nc = self.chunks[i]
        return self.fulls[a].at[(*where, slice(r, r + nr), slice(c, c + nc))]

    def own(self, i):
        return pltpu.make_async_copy(self.piece(i), self.full(i, *self.where), self.own_sem.at[i])

    def along_z(self, i, k):
        s, z, y, x = self.where
        return remote(
            self.piece(i),
            self.full(i, s, z, y, x),
            self.send.at[i, k - 1],
            self.recv.at[i, k - 1],
            device(s, (z + k) % 4, y, x),
        )

    def first(self, i):
        s, z, y, x = self.where
        part = self.full(i, s, slice(None), y, x)
        return remote(
            part, part, self.send.at[i, 3], self.recv.at[i, 3], second_partner(s, z, y, x)
        )

    def second(self, i, j):
        s, z, y, x = self.where
        yy = y * (1 - s) + j * s
        xx = j * (1 - s) + x * s
        part = self.full(i, s, slice(None), yy, xx)
        return remote(
            part, part, self.send.at[i, 4 + j], self.recv.at[i, 4 + j], first_partner(s, z, y, x)
        )

    def across(self, i):
        s, z, y, x = self.where
        part = self.full(i, s, slice(None), slice(None), slice(None))
        return remote(part, part, self.send.at[i, 6], self.recv.at[i, 6], device(1 - s, z, y, x))

    def stage(self, t, i):
        if not 0 <= i < len(self.chunks):
            return
        if t == 0:
            for k in (1, 2, 3):
                self.along_z(i, k).start()
            self.own(i).start()
        elif t == 1:
            self.own(i).wait()
            for k in (1, 2, 3):
                self.along_z(i, k).wait_recv()
            self.first(i).start()
        elif t == 2:
            self.first(i).wait_recv()
            for j in (0, 1):
                self.second(i, j).start()
        elif t == 3:
            for j in (0, 1):
                self.second(i, j).wait_recv()
            self.across(i).start()

    def begin(self):
        for i in range(AHEAD):
            self.stage(0, i)

    def steps(self):
        return len(self.chunks) + 2 * LAG

    def step(self, n):
        self.stage(3, n - 2 * LAG)
        self.stage(2, n - LAG)
        self.stage(1, n)
        self.stage(0, n + AHEAD)

    def sent(self):
        for i in range(len(self.chunks)):
            for k in (1, 2, 3):
                self.along_z(i, k).wait_send()
            self.first(i).wait_send()
            for j in (0, 1):
                self.second(i, j).wait_send()
            self.across(i).wait_send()


class Scatter:
    def __init__(self, terms, held, gots, outs, load, send, recv, chunks, where):
        self.terms, self.held, self.gots, self.outs, self.chunks = terms, held, gots, outs, chunks
        self.load, self.send, self.recv, self.where = load, send, recv, where

    def cut(self, refs, i, *where):
        a, r, nr, c, nc = self.chunks[i]
        return refs[a].at[(*where, slice(r, r + nr), slice(c, c + nc))]

    def out(self, i):
        a, r, nr, c, nc = self.chunks[i]
        return self.outs[a].at[r : r + nr, c : c + nc]

    def fetch(self, i):
        s = self.where[0]
        every = (slice(None),) * 3
        return pltpu.make_async_copy(
            self.cut(self.terms, i, s, *every), self.cut(self.held, i, *every), self.load.at[i]
        )

    def fetched(self, i):
        return self.load is not None and i < self.load.shape[0]

    def across(self, i):
        s, z, y, x = self.where
        every = (slice(None),) * 3
        return remote(
            self.cut(self.terms, i, 1 - s, *every),
            self.cut(self.gots[0], i, *every),
            self.send.at[i, 0],
            self.recv.at[i, 0],
            device(1 - s, z, y, x),
        )

    def first(self, i, j):
        s, z, y, x = self.where
        yy = (1 - y) * (1 - s) + j * s
        xx = j * (1 - s) + (1 - x) * s
        return remote(
            self.cut(self.held, i, slice(None), yy, xx),
            self.cut(self.gots[1], i, slice(None), j),
            self.send.at[i, 1 + j],
            self.recv.at[i, 1 + j],
            first_partner(s, z, y, x),
        )

    def second(self, i):
        s, z, y, x = self.where
        y2 = y * (1 - s) + (1 - y) * s
        x2 = (1 - x) * (1 - s) + x * s
        return remote(
            self.cut(self.held, i, slice(None), y2, x2),
            self.cut(self.gots[2], i, slice(None)),
            self.send.at[i, 3],
            self.recv.at[i, 3],
            second_partner(s, z, y, x),
        )

    def along_z(self, i, k):
        s, z, y, x = self.where
        zt = (z + k) % 4
        return remote(
            self.cut(self.held, i, zt, y, x),
            self.cut(self.gots[3], i, k - 1),
            self.send.at[i, 3 + k],
            self.recv.at[i, 3 + k],
            device(s, zt, y, x),
        )

    def add(self, to, term):
        to[...] = to[...] + term[...]

    def stage(self, t, i):
        s, z, y, x = self.where
        if t == 0:
            self.across(i).start()
            if self.fetched(i):
                self.fetch(i).start()
        elif t == 1:
            if self.fetched(i):
                self.fetch(i).wait()
            self.across(i).wait_recv()

            def add1(n, unused):
                at = (n // 4, (n // 2) % 2, n % 2)
                self.add(self.cut(self.held, i, *at), self.cut(self.gots[0], i, *at))
                return unused

            lax.fori_loop(0, 16, add1, 0)
            for j in (0, 1):
                self.first(i, j).start()
        elif t == 2:
            for j in (0, 1):
                self.first(i, j).wait_recv()

            def add2(n, unused):
                zz, j = n // 2, n % 2
                yy = y * (1 - s) + j * s
                xx = j * (1 - s) + x * s
                self.add(self.cut(self.held, i, zz, yy, xx), self.cut(self.gots[1], i, zz, j))
                return unused

            lax.fori_loop(0, 8, add2, 0)
            self.second(i).start()
        elif t == 3:
            self.second(i).wait_recv()

            def add3(zz, unused):
                self.add(self.cut(self.held, i, zz, y, x), self.cut(self.gots[2], i, zz))
                return unused

            lax.fori_loop(0, 4, add3, 0)
            for k in (1, 2, 3):
                self.along_z(i, k).start()
        elif t == 4:
            for k in (1, 2, 3):
                self.along_z(i, k).wait_recv()
            total = self.cut(self.held, i, z, y, x)[...].astype(F32)
            for k in (0, 1, 2):
                total = total + self.cut(self.gots[3], i, k)[...].astype(F32)
            self.out(i)[...] = total

    def sent(self):
        for i in range(len(self.chunks)):
            self.across(i).wait_send()
            for j in (0, 1):
                self.first(i, j).wait_send()
            self.second(i).wait_send()
            for k in (1, 2, 3):
                self.along_z(i, k).wait_send()


def got_shapes(sizes):
    return [pltpu.VMEM(lead + size, BF16) for lead in ((4, 2, 2), (4, 2), (4,), (3,)) for size in sizes]


def got_levels(refs, count):
    return [refs[level * count : (level + 1) * count] for level in range(4)]


def head_of(shape):
    return lax.broadcasted_iota(jnp.int32, shape, len(shape) - 1) // 64


def pick(values, head):
    return jnp.where(head_of(values.shape) == head, values, jnp.zeros_like(values))


def attend_pair(queries, keys, values):
    length = queries.shape[0]
    mixed, logs = [], []
    for head in (0, 1):
        scores = dot_nt(pick(queries, head), keys)
        top = jnp.max(scores, axis=1, keepdims=True)
        powers = jnp.exp(scores - top)
        total = jnp.sum(powers, axis=1, keepdims=True)
        mixed.append(dot_nn(powers.astype(BF16), values) * (1.0 / total))
        column = jnp.broadcast_to(top + jnp.log(total), (length, LANES))
        logs.append(jnp.transpose(column)[0:1])
    attended = jnp.where(head_of(mixed[0].shape) == 0, mixed[0], mixed[1]).astype(BF16)
    return attended, jnp.concatenate(logs, axis=0)


def attend_pair_back(queries, keys, values, attended, grad, logs):
    keys_t = jnp.transpose(keys)
    products = jnp.transpose(grad.astype(F32) * attended.astype(F32))
    dk = jnp.zeros(keys.shape, F32)
    dv = jnp.zeros(keys.shape, F32)
    dq_t = []
    for head in (0, 1):
        offset = jnp.sum(products[64 * head : 64 * head + 64], axis=0, keepdims=True)
        q_head = pick(queries, head)
        g_head = pick(grad, head)
        scores_t = dot_nt(keys, q_head)
        probs_t = jnp.exp(scores_t - logs[head : head + 1, :])
        slopes_t = dot_nt(values, g_head)
        score_grad_t = (probs_t * (slopes_t - offset)).astype(BF16)
        dv += dot_nn(probs_t.astype(BF16), g_head)
        dk += dot_nn(score_grad_t, q_head)
        dq_t.append(dot_nn(keys_t[64 * head : 64 * head + 64], score_grad_t))
    dq = jnp.transpose(jnp.concatenate(dq_t, axis=0)) * SCALE
    return dq.astype(BF16), dk.astype(BF16), dv.astype(BF16)


def attend_kernel(q_ref, k_ref, v_ref, o_ref, lse_ref):
    keys = k_ref[:, 0].reshape(-1, PAIR)
    values = v_ref[:, 0].reshape(-1, PAIR)
    o_ref[0], lse_ref[0, 0] = attend_pair(q_ref[0], keys, values)


def attend(queries, keys, values):
    micro, length, width = queries.shape
    parts = keys.shape[0]
    pairs = width // PAIR
    row = pl.BlockSpec((1, length, PAIR), lambda m, p: (m, 0, p))
    col = pl.BlockSpec((parts, 1, length, PAIR), lambda m, p: (0, m, 0, p))
    return pl.pallas_call(
        attend_kernel,
        grid=(micro, pairs),
        in_specs=[row, col, col],
        out_specs=[row, pl.BlockSpec((1, 1, 2, length), lambda m, p: (m, p, 0, 0))],
        out_shape=[
            jax.ShapeDtypeStruct(queries.shape, BF16),
            jax.ShapeDtypeStruct((micro, pairs, 2, length), F32),
        ],
        compiler_params=pltpu.CompilerParams(vmem_limit_bytes=VMEM_LIMIT),
        name="attend",
    )(queries, keys, values)


def attend_back_kernel(q_ref, k_ref, v_ref, o_ref, g_ref, lse_ref, dq_ref, dk_ref, dv_ref):
    parts, length = k_ref.shape[0], q_ref.shape[1]
    keys = k_ref[:, 0].reshape(-1, PAIR)
    values = v_ref[:, 0].reshape(-1, PAIR)
    dq, dk, dv = attend_pair_back(q_ref[0], keys, values, o_ref[0], g_ref[0], lse_ref[0, 0])
    dq_ref[0] = dq
    dk_ref[:, 0] = dk.reshape(parts, length, PAIR)
    dv_ref[:, 0] = dv.reshape(parts, length, PAIR)


def attend_back(queries, keys, values, attended, grad, lse):
    micro, length, width = queries.shape
    parts = keys.shape[0]
    pairs = width // PAIR
    row = pl.BlockSpec((1, length, PAIR), lambda m, p: (m, 0, p))
    col = pl.BlockSpec((parts, 1, length, PAIR), lambda m, p: (0, m, 0, p))
    log = pl.BlockSpec((1, 1, 2, length), lambda m, p: (m, p, 0, 0))
    return pl.pallas_call(
        attend_back_kernel,
        grid=(micro, pairs),
        in_specs=[row, col, col, row, row, log],
        out_specs=[row, col, col],
        out_shape=[
            jax.ShapeDtypeStruct((micro, length, width), BF16),
            jax.ShapeDtypeStruct((parts, micro, length, width), BF16),
            jax.ShapeDtypeStruct((parts, micro, length, width), BF16),
        ],
        compiler_params=pltpu.CompilerParams(vmem_limit_bytes=VMEM_LIMIT),
        name="attend_back",
    )(queries, keys, values, attended, grad, lse)


def project_kernel(own_ref, all_ref, wq_ref, wk_ref, wv_ref, small_ref, q_ref, k_ref, v_ref, bias):
    @pl.when(pl.program_id(0) == 0)
    def _():
        bias[...] = spread(small_ref[:, 0:8].astype(F32), bias.shape[1])

    @pl.when(pl.program_id(0) < own_ref.shape[0] * 2)
    def _():
        queries = dot_nn(own_ref[0], wq_ref[...]) + bias[0:1]
        q_ref[0] = (queries.astype(BF16).astype(F32) * SCALE).astype(BF16)

    rows = all_ref[0, 0]
    k_ref[0, 0] = dot_nn(rows, wk_ref[...]).astype(BF16)
    v_ref[0, 0] = (dot_nn(rows, wv_ref[...]) + bias[1:2]).astype(BF16)


def project(own, all_rows, wq, wk, wv, small):
    micro, length, width = own.shape
    parts = all_rows.shape[0]
    whole = lambda a: pl.BlockSpec(a.shape, lambda i: (0,) * a.ndim)
    last = micro - 1
    mine = pl.BlockSpec((1, length, width), lambda i: (jnp.minimum(i, last), 0, 0))
    every = pl.BlockSpec((1, 1, length, width), lambda i: (i // micro, i % micro, 0, 0))
    return pl.pallas_call(
        project_kernel,
        grid=(parts * micro,),
        in_specs=[mine, every, whole(wq), whole(wk), whole(wv), whole(small)],
        out_specs=[mine, every, every],
        out_shape=[
            jax.ShapeDtypeStruct((micro, length, width), BF16),
            jax.ShapeDtypeStruct((parts, micro, length, width), BF16),
            jax.ShapeDtypeStruct((parts, micro, length, width), BF16),
        ],
        scratch_shapes=[pltpu.VMEM((8, width), F32)],
        compiler_params=pltpu.CompilerParams(vmem_limit_bytes=VMEM_LIMIT),
        name="project",
    )(own, all_rows, wq, wk, wv, small)


SMALL, WQ, WK, WV, WO, WIN, WOUT = range(7)


def forward_chunks(shapes):
    chunks = [(SMALL, 0, shapes[SMALL][0], 0, LANES)]
    rows, width = shapes[WQ]
    for c in range(0, width, GROUP):
        chunks += [(w, 0, rows, c, GROUP) for w in (WQ, WK, WV)]
    chunks.append((WO, 0, rows, 0, width))
    chunks += [(WIN, 0, rows, c, CHUNK) for c in range(0, shapes[WIN][1], CHUNK)]
    chunks += [(WOUT, 0, shapes[WOUT][0], c, GROUP) for c in range(0, width, GROUP)]
    return chunks


def forward_kernel(chunks, *refs):
    shards, x_ref, fulls = refs[:7], refs[7], refs[8:15]
    q_out, k_out, v_out, att_ref, lse_ref = refs[15:20]
    other, pieces, weights, small, bias, q_s, k_s, v_s = refs[20:28]
    own_sem, send, recv, row_send, row_recv, load, back = refs[28:]
    where = place()
    s, z, y, x = where
    width = q_s.shape[2]
    length = q_s.shape[1]
    groups = width // GROUP
    greet(s, z, y, x)
    gather = Gather(shards, fulls, own_sem, send, recv, chunks, where)
    rows = remote(x_ref, other, row_send, row_recv, device(1 - s, z, y, x))
    gather.begin()
    rows.start()

    def fetch(g):
        copies = []
        for n, w in enumerate((WQ, WK, WV)):
            source = fulls[w].at[:, :, :, :, :, g * GROUP : (g + 1) * GROUP]
            target = pieces.at[:, :, :, :, :, n * GROUP : (n + 1) * GROUP]
            copies.append(pltpu.make_async_copy(source, target, load.at[n]))
        return copies

    def arrived(g):
        for i in range(3 * g + 1, 3 * g + 4):
            gather.across(i).wait_recv()
        for copy in fetch(g):
            copy.start()

    def written(g):
        cols = slice(g * GROUP, (g + 1) * GROUP)
        return [
            pltpu.make_async_copy(q_s.at[:, :, cols], q_out.at[:, :, cols], back.at[g, 0]),
            pltpu.make_async_copy(k_s.at[:, :, :, cols], k_out.at[:, :, :, cols], back.at[g, 1]),
            pltpu.make_async_copy(v_s.at[:, :, :, cols], v_out.at[:, :, :, cols], back.at[g, 2]),
        ]

    ready = 4 + 2 * LAG
    for n in range(ready):
        gather.step(n)
    gather.across(0).wait_recv()
    small_copy = pltpu.make_async_copy(fulls[SMALL], small, load.at[3])
    small_copy.start()
    arrived(0)
    small_copy.wait()
    vectors = small[...].reshape(32, 16, LANES)[:, 0:8]
    bias[...] = spread(vectors.astype(F32), width)
    rows.wait_recv()

    for g in range(groups):
        for copy in fetch(g):
            copy.wait()
        weights[...] = pieces[...].reshape(weights.shape)
        cols = slice(g * GROUP, (g + 1) * GROUP)

        def mine(m, unused):
            made = dot_nn(x_ref[m], weights[...])
            queries = made[:, :GROUP] + bias[0:1, cols]
            q_s[m, :, cols] = (queries.astype(BF16).astype(F32) * SCALE).astype(BF16)
            k_s[0, m, :, cols] = made[:, GROUP : 2 * GROUP].astype(BF16)
            v_s[0, m, :, cols] = (made[:, 2 * GROUP :] + bias[1:2, cols]).astype(BF16)
            return unused

        def others(m, unused):
            made = dot_nn(other[m], weights[:, GROUP:])
            k_s[1, m, :, cols] = made[:, :GROUP].astype(BF16)
            v_s[1, m, :, cols] = (made[:, GROUP:] + bias[1:2, cols]).astype(BF16)
            return unused

        lax.fori_loop(0, 2, mine, 0)
        lax.fori_loop(0, 2, others, 0)
        for copy in written(g):
            copy.start()

        def one(j, unused):
            for n in range(3):

                @pl.when(j == n)
                def _():
                    gather.step(ready + 3 * g + n)

            if g + 1 < groups:

                @pl.when(j == 3)
                def _():
                    arrived(g + 1)

            m = j // 2
            p = 2 * g + j % 2
            lanes = pl.ds(pl.multiple_of(p * PAIR, PAIR), PAIR)
            keys = k_s[:, m, :, lanes].reshape(2 * length, PAIR)
            values = v_s[:, m, :, lanes].reshape(2 * length, PAIR)
            attended, logs = attend_pair(q_s[m, :, lanes], keys, values)
            att_ref[m, :, lanes] = attended
            lse_ref[m, p] = logs
            return unused

        lax.fori_loop(0, 4, one, 0)

    for n in range(ready + 3 * groups, gather.steps()):
        gather.step(n)
    for i in range(3 * groups + 1, len(chunks)):
        gather.across(i).wait_recv()
    for g in range(groups):
        for copy in written(g):
            copy.wait()
    rows.wait_send()
    gather.sent()


def forward_box(shards, own):
    micro, length, width = own.shape
    chunks = forward_chunks([a.shape for a in shards])
    any_spec = pl.BlockSpec(memory_space=pl.ANY)
    vmem_spec = pl.BlockSpec(memory_space=pltpu.VMEM)
    count = len(chunks)
    pairs = width // PAIR
    twice = (2, micro, length, width)
    outs = pl.pallas_call(
        functools.partial(forward_kernel, chunks),
        out_shape=[jax.ShapeDtypeStruct((2, 4, 2, 2) + a.shape, a.dtype) for a in shards]
        + [
            jax.ShapeDtypeStruct(own.shape, BF16),
            jax.ShapeDtypeStruct(twice, BF16),
            jax.ShapeDtypeStruct(twice, BF16),
            jax.ShapeDtypeStruct(own.shape, BF16),
            jax.ShapeDtypeStruct((micro, pairs, 2, length), F32),
        ],
        in_specs=[vmem_spec] * 8,
        out_specs=[any_spec] * 10 + [vmem_spec] * 2,
        scratch_shapes=[
            pltpu.VMEM(own.shape, BF16),
            pltpu.VMEM((2, 4, 2, 2, width // 32, 3 * GROUP), BF16),
            pltpu.VMEM((width, 3 * GROUP), BF16),
            pltpu.VMEM((2, 4, 2, 2, 16, LANES), BF16),
            pltpu.VMEM((8, width), F32),
            pltpu.VMEM(own.shape, BF16),
            pltpu.VMEM(twice, BF16),
            pltpu.VMEM(twice, BF16),
            pltpu.SemaphoreType.DMA((count,)),
            pltpu.SemaphoreType.DMA((count, 7)),
            pltpu.SemaphoreType.DMA((count, 7)),
            pltpu.SemaphoreType.DMA,
            pltpu.SemaphoreType.DMA,
            pltpu.SemaphoreType.DMA((4,)),
            pltpu.SemaphoreType.DMA((width // GROUP, 3)),
        ],
        compiler_params=pltpu.CompilerParams(
            collective_id=1, has_side_effects=True, vmem_limit_bytes=VMEM_LIMIT
        ),
        name="forward_attention",
    )(*shards, own)
    fulls = [full.reshape((-1, full.shape[-1])) for full in outs[1:7]]
    return [outs[0].reshape(32, 16, LANES)] + fulls, outs[7:]


def mean_rows(values):
    return jnp.mean(values, axis=-1, keepdims=True)


def rows_kernel(
    x_ref,
    att_ref,
    cot_ref,
    wo_ref,
    win_ref,
    wout_ref,
    small_ref,
    out_ref,
    hidden_ref,
    active_ref,
    inner_grad_ref,
    feed_ref,
    branch_ref,
    mixed_ref,
    first_ref,
    smallg_ref,
    vec,
    ib,
    slope,
    vecg,
    ibg,
):
    step = pl.program_id(0)
    chunks = win_ref.shape[1] // CHUNK

    @pl.when(step == 0)
    def _():
        vec[...] = spread(small_ref[:, 0:8].astype(F32), vec.shape[1])
        ib[...] = spread(small_ref[:, 8:16].astype(F32), ib.shape[1])
        vecg[...] = jnp.zeros_like(vecg)
        ibg[...] = jnp.zeros_like(ibg)

    o_b, g1, s1, outer_b, g2, s2 = (vec[i : i + 1] for i in range(2, 8))
    first_sum = x_ref[...].astype(F32) + (dot_nn(att_ref[...], wo_ref[...]) + o_b)
    centred = first_sum - mean_rows(first_sum)
    r1 = lax.rsqrt(mean_rows(centred * centred) + EPS)
    n1 = centred * r1
    hidden = n1 * g1 + s1
    hidden_low = hidden.astype(BF16)
    hidden_ref[...] = hidden_low
    total = hidden + outer_b
    for c in range(chunks):
        cols = slice(c * CHUNK, (c + 1) * CHUNK)
        v = dot_nn(hidden_low, win_ref[:, cols]) + ib[0:1, cols]
        square = v * v
        t = jnp.tanh(v * (GELU_C + (GELU_C * GELU_A) * square))
        half = 0.5 * (1.0 + t)
        active = (v * half).astype(BF16)
        active_ref[:, cols] = active
        slope[:, cols] = half + (0.5 * v) * (1.0 - t * t) * (
            GELU_C + (3.0 * GELU_C * GELU_A) * square
        )
        total = total + dot_nn(active, wout_ref[cols, :])
    centred = total - mean_rows(total)
    r2 = lax.rsqrt(mean_rows(centred * centred) + EPS)
    n2 = centred * r2
    out_ref[...] = (n2 * g2 + s2).astype(BF16)
    e = cot_ref[...].astype(F32)
    m = e * g2
    second = (m - mean_rows(m) - n2 * mean_rows(m * n2)) * r2
    feed = second.astype(BF16)
    feed_ref[...] = feed
    vecg[6:7] += jnp.sum(e * n2, axis=0, keepdims=True)
    vecg[7:8] += jnp.sum(e, axis=0, keepdims=True)
    vecg[5:6] += jnp.sum(feed.astype(F32), axis=0, keepdims=True)
    e = second
    for c in range(chunks):
        cols = slice(c * CHUNK, (c + 1) * CHUNK)
        inner_grad = (dot_nt(feed, wout_ref[cols, :]) * slope[:, cols]).astype(BF16)
        inner_grad_ref[:, cols] = inner_grad
        ibg[0:1, cols] += jnp.sum(inner_grad.astype(F32), axis=0, keepdims=True)
        e = e + dot_nt(inner_grad, win_ref[:, cols])
    m = e * g1
    first = (m - mean_rows(m) - n1 * mean_rows(m * n1)) * r1
    first_ref[...] = first
    branch = first.astype(BF16)
    branch_ref[...] = branch
    vecg[3:4] += jnp.sum(e * n1, axis=0, keepdims=True)
    vecg[4:5] += jnp.sum(e, axis=0, keepdims=True)
    vecg[2:3] += jnp.sum(branch.astype(F32), axis=0, keepdims=True)
    mixed_ref[...] = dot_nt(branch, wo_ref[...]).astype(BF16)

    @pl.when(step == pl.num_programs(0) - 1)
    def _():
        devices = smallg_ref.shape[0]
        smallg_ref[:, 0:8] = collect(vecg[...], devices).astype(BF16)
        smallg_ref[:, 8:16] = collect(ibg[...], devices).astype(BF16)


def row_stage(x, attended, cotangent, wo, win, wout, small):
    rows, width = x.shape
    hidden_width = win.shape[1]
    block = min(ROWS, rows)
    whole = lambda a: pl.BlockSpec(
        a.shape, lambda i: (0,) * a.ndim, pipeline_mode=pl.Buffered(1)
    )
    narrow = pl.BlockSpec((block, width), lambda i: (i, 0))
    wide = pl.BlockSpec((block, hidden_width), lambda i: (i, 0))
    low = jax.ShapeDtypeStruct((rows, width), BF16)
    low_wide = jax.ShapeDtypeStruct((rows, hidden_width), BF16)
    return pl.pallas_call(
        rows_kernel,
        grid=(rows // block,),
        in_specs=[narrow] * 3 + [whole(a) for a in (wo, win, wout, small)],
        out_specs=[
            narrow,
            narrow,
            wide,
            wide,
            narrow,
            narrow,
            narrow,
            narrow,
            pl.BlockSpec(small.shape, lambda i: (0, 0, 0)),
        ],
        out_shape=[
            low,
            low,
            low_wide,
            low_wide,
            low,
            low,
            low,
            jax.ShapeDtypeStruct((rows, width), F32),
            jax.ShapeDtypeStruct(small.shape, BF16),
        ],
        scratch_shapes=[
            pltpu.VMEM((8, width), F32),
            pltpu.VMEM((8, hidden_width), F32),
            pltpu.VMEM((block, hidden_width), F32),
            pltpu.VMEM((8, width), F32),
            pltpu.VMEM((8, hidden_width), F32),
        ],
        compiler_params=pltpu.CompilerParams(vmem_limit_bytes=VMEM_LIMIT),
        name="row_stage",
    )(x, attended, cotangent, wo, win, wout, small)


def product_kernel(left_ref, right_ref, out_ref):
    out_ref[...] = dot_tn(left_ref[...], right_ref[...]).astype(BF16)


def product(left, right, block_m, block_n):
    depth, rows = left.shape
    cols = right.shape[1]
    return pl.pallas_call(
        product_kernel,
        grid=(rows // block_m, cols // block_n),
        in_specs=[
            pl.BlockSpec((depth, block_m), lambda i, j: (0, i)),
            pl.BlockSpec((depth, block_n), lambda i, j: (0, j)),
        ],
        out_specs=pl.BlockSpec((block_m, block_n), lambda i, j: (i, j)),
        out_shape=jax.ShapeDtypeStruct((rows, cols), BF16),
        compiler_params=pltpu.CompilerParams(vmem_limit_bytes=VMEM_LIMIT),
        name="weight_gradient",
    )(left, right)


def input_kernel(first_ref, dq_ref, dk_ref, dv_ref, wq_ref, wk_ref, wv_ref, out_ref, vecg_ref, acc):
    step = pl.program_id(0)

    @pl.when(step == 0)
    def _():
        acc[...] = jnp.zeros_like(acc)

    out_ref[...] = (
        first_ref[...]
        + dot_nt(dq_ref[...], wq_ref[...])
        + dot_nt(dk_ref[...], wk_ref[...])
        + dot_nt(dv_ref[...], wv_ref[...])
    ).astype(BF16)
    acc[0:1] += jnp.sum(dq_ref[...].astype(F32), axis=0, keepdims=True)
    acc[1:2] += jnp.sum(dv_ref[...].astype(F32), axis=0, keepdims=True)

    @pl.when(step == pl.num_programs(0) - 1)
    def _():
        vecg_ref[:, 0:8] = collect(acc[...], vecg_ref.shape[0]).astype(BF16)
        vecg_ref[:, 8:16] = jnp.zeros((vecg_ref.shape[0], 8, LANES), BF16)


def input_stage(first, dq, dk, dv, wq, wk, wv, small_shape):
    rows, width = first.shape
    block = min(ROWS, rows)
    narrow = pl.BlockSpec((block, width), lambda i: (i, 0))
    whole = pl.BlockSpec((width, width), lambda i: (0, 0))
    return pl.pallas_call(
        input_kernel,
        grid=(rows // block,),
        in_specs=[narrow] * 4 + [whole] * 3,
        out_specs=[narrow, pl.BlockSpec(small_shape, lambda i: (0, 0, 0))],
        out_shape=[
            jax.ShapeDtypeStruct((rows, width), BF16),
            jax.ShapeDtypeStruct(small_shape, BF16),
        ],
        scratch_shapes=[pltpu.VMEM((8, width), F32)],
        compiler_params=pltpu.CompilerParams(vmem_limit_bytes=VMEM_LIMIT),
        name="input_stage",
    )(first, dq, dk, dv, wq, wk, wv)


PLAN_IN = ((1, 2, 6, 9, 11), (1, 4, 6, 8, 18), (1, 2, 5, 7, 19), (0, 1, 9, 11, 16),)
PLAN_OUT = ((0, 1, 5, 9, 19), (9, 10, 13, 15, 17), (2, 8, 11, 13, 19))
PLAN_O, PLAN_SMALL, PLAN_SMALL2 = (2, 5, 9, 10, 19), (5, 6, 9, 10, 19), (13, 15, 16, 18, 24)
PLAN_QKV = (
    (6, 7, 10, 12, 19),
    (10, 11, 14, 16, 23),
    (13, 14, 16, 20, 23),
    (13, 15, 20, 21, 24),
)
G_IN, G_OUT, G_O, G_SMALL, G_QKV, G_SMALL2 = 0, 1, 2, 3, 4, 8
UNITS = 12
BACK_STEPS = UNITS + 5
BACK_PLAN = (
    [(G_OUT, c * GROUP, GROUP, plan) for c, plan in enumerate(PLAN_OUT)]
    + [(G_IN, c * CHUNK, CHUNK, plan) for c, plan in enumerate(PLAN_IN)]
    + [(G_O, 0, CHUNK, PLAN_O), (G_SMALL, 0, LANES, PLAN_SMALL)]
    + [(G_QKV + g, 0, 3 * w, plan) for g, (w, plan) in enumerate(zip((256, 256, 128, 128), PLAN_QKV))]
    + [(G_SMALL2, 0, LANES, PLAN_SMALL2)]
)
FETCHED = 9


def unit_of(step):
    u = jnp.clip(step, 0, UNITS - 1)
    return u % 2, u // 2


def backward_kernel(sizes, *refs):
    terms1 = refs[:4]
    (q_ref, k_ref, v_ref, o_ref, g_ref, lse_ref, x_in, wq_in, wk_in, wv_in, first_ref) = refs[4:15]
    outs, dx_ref = refs[15:24], refs[24]
    held1 = refs[25:29]
    broad, slim, small2, sums = refs[29:33]
    gots = got_levels(refs[33:69], 9)
    dq_all, dk_all, dv_all, away, far, x_t, x_v, wq_v, wk_v, wv_v = refs[69:79]
    load, send, recv, far_send, far_recv, bring = refs[79:]
    where = place()
    s, z, y, x = where
    step = pl.program_id(0)
    length = q_ref.shape[1]
    rows = dq_all.shape[0] * length
    chunks = [(a, 0, sizes[a][0], c, nc) for a, c, nc, _ in BACK_PLAN]
    terms = list(terms1) + [a.at[g] for a in (broad, slim) for g in (0, 1)] + [small2]
    held = list(held1) + [a.at[g, s] for a in (broad, slim) for g in (0, 1)] + [small2.at[s]]
    scatter = Scatter(terms, held, gots, outs, load, send, recv, chunks, where)
    copies = [
        pltpu.make_async_copy(a, b, bring.at[n])
        for n, (a, b) in enumerate(zip((x_in, wq_in, wk_in, wv_in), (x_v, wq_v, wk_v, wv_v)))
    ]

    def far_copies(u):
        m, p = unit_of(u)
        lanes = pl.ds(pl.multiple_of(p * PAIR, PAIR), PAIR)
        target = device(1 - s, z, y, x)
        return [
            remote(
                away.at[u, n], far.at[n, m, :, lanes], far_send.at[u, n], far_recv.at[u, n], target
            )
            for n in (0, 1)
        ]

    @pl.when(step == 0)
    def _():
        for copy in copies:
            copy.start()
        greet(s, z, y, x)

    for n in range(BACK_STEPS):
        todo = [(t, i) for i, c in enumerate(BACK_PLAN) for t, at in enumerate(c[3]) if at == n]
        if todo:

            @pl.when(step == n)
            def _():
                for t, i in sorted(todo, reverse=True):
                    scatter.stage(t, i)

    @pl.when((step > 0) & (step < UNITS))
    def _():
        for copy in far_copies(step - 1):
            copy.start()

    @pl.when(step == 1)
    def _():
        copies[0].wait()
        x_t[...] = jnp.transpose(x_v[...])

    @pl.when(step < UNITS)
    def _():
        m, p = unit_of(step)
        lanes = pl.ds(pl.multiple_of(p * PAIR, PAIR), PAIR)
        keys = k_ref[:, 0].reshape(-1, PAIR)
        values = v_ref[:, 0].reshape(-1, PAIR)
        dq, dk, dv = attend_pair_back(q_ref[0], keys, values, o_ref[0], g_ref[0], lse_ref[0, 0])
        dq_all[m, :, lanes] = dq
        dk_all[m, :, lanes] = dk[:length]
        dv_all[m, :, lanes] = dv[:length]
        away[step, 0] = dk[length:]
        away[step, 1] = dv[length:]

    @pl.when(step == UNITS)
    def _():
        for copy in far_copies(UNITS - 1):
            copy.start()

    def products(to, g, unit, units, lane, lanes):
        for n in range(units):
            for copy in far_copies(unit + n):
                copy.wait_recv()
        cols = pl.ds(pl.multiple_of(lane, PAIR), lanes)
        for m in range(dq_all.shape[0]):
            for n, whole in enumerate((dk_all, dv_all)):
                whole[m, :, cols] = whole[m, :, cols] + far[n, m, :, cols]
        for n, whole in enumerate((dq_all, dk_all, dv_all)):
            value = dot_nn(x_t[...], whole[:, :, cols].reshape(rows, lanes)).astype(BF16)
            to[g, :, :, :, :, :, n * lanes : (n + 1) * lanes] = value.reshape(
                (2, 4, 2, 2) + (sizes[G_QKV][0], lanes)
            )

    @pl.when((step == 5) | (step == 9))
    def _():
        g = (step - 5) // 4
        products(broad, g, 4 * g, 4, g * GROUP, GROUP)

    @pl.when((step == 11) | (step == 12))
    def _():
        g = step - 11
        products(slim, g, 8 + 2 * g, 2, 2 * GROUP + g * PAIR, PAIR)

    @pl.when(step == UNITS)
    def _():
        sums[...] = jnp.zeros_like(sums)
        for n, whole in enumerate((dq_all, dv_all)):
            total = jnp.sum(whole[...].astype(F32).reshape(rows, -1), axis=0, keepdims=True)
            sums[n : n + 1] = total
        small2[...] = jnp.zeros_like(small2)
        small2[:, :, :, :, 0:8] = (
            collect(sums[...], 32).astype(BF16).reshape((2, 4, 2, 2, 8, LANES))
        )
        for copy in copies[1:]:
            copy.wait()

    @pl.when(step > UNITS)
    def _():
        block = first_ref.shape[0]
        r = step - UNITS - 1
        per = length // block
        at = pl.ds(pl.multiple_of((r % per) * block, block), block)
        dx_ref[...] = (
            first_ref[...]
            + dot_nt(dq_all[r // per, at], wq_v[...])
            + dot_nt(dk_all[r // per, at], wk_v[...])
            + dot_nt(dv_all[r // per, at], wv_v[...])
        ).astype(BF16)

    @pl.when(step == BACK_STEPS - 1)
    def _():
        late = [(at, -t, i) for i, c in enumerate(BACK_PLAN) for t, at in enumerate(c[3])]
        for at, t, i in sorted(late):
            if at >= BACK_STEPS:
                scatter.stage(-t, i)
        for u in range(UNITS):
            for copy in far_copies(u):
                copy.wait_send()
        scatter.sent()


def backward_box(win_grad, wout_grad, wo_grad, small, q, k, v, o, g, lse, tokens, wq, wk, wv, first):
    micro, length, width = q.shape
    rows = tokens.shape[0]
    narrow, thin = (width // 32, width), (16, LANES)
    sizes = [(width // 32, win_grad.shape[1]), (wout_grad.shape[0] // 32, width), narrow, thin]
    sizes += [(narrow[0], 3 * w) for w in (GROUP, GROUP, PAIR, PAIR)] + [thin]
    terms = [
        a.reshape((2, 4, 2, 2) + size)
        for a, size in zip((win_grad, wout_grad, wo_grad, small), sizes)
    ]
    block = rows // 4

    def at(i):
        return unit_of(i)

    row = pl.BlockSpec((1, length, PAIR), lambda i: (at(i)[0], 0, at(i)[1]))
    col = pl.BlockSpec((2, 1, length, PAIR), lambda i: (0, at(i)[0], 0, at(i)[1]))
    log = pl.BlockSpec((1, 1, 2, length), lambda i: (at(i)[0], at(i)[1], 0, 0))
    flat = pl.BlockSpec((block, width), lambda i: (jnp.clip(i - UNITS - 1, 0, 3), 0))
    any_spec = pl.BlockSpec(memory_space=pl.ANY)
    square = pltpu.VMEM((width, width), BF16)
    low = pltpu.VMEM((micro, length, width), BF16)
    outs = pl.pallas_call(
        functools.partial(backward_kernel, sizes),
        grid=(BACK_STEPS,),
        in_specs=[any_spec] * 4 + [row, col, col, row, row, log] + [any_spec] * 4 + [flat],
        out_specs=[pl.BlockSpec(size, lambda i: (0, 0)) for size in sizes] + [flat],
        out_shape=[jax.ShapeDtypeStruct(size, F32) for size in sizes]
        + [jax.ShapeDtypeStruct((rows, width), BF16)],
        scratch_shapes=[pltpu.VMEM((4, 2, 2) + size, BF16) for size in sizes[:4]]
        + [
            pltpu.VMEM((2, 2, 4, 2, 2) + sizes[G_QKV], BF16),
            pltpu.VMEM((2, 2, 4, 2, 2) + sizes[G_QKV + 2], BF16),
            pltpu.VMEM((2, 4, 2, 2) + thin, BF16),
            pltpu.VMEM((8, width), F32),
        ]
        + got_shapes(sizes)
        + [
            low,
            low,
            low,
            pltpu.VMEM((UNITS, 2, length, PAIR), BF16),
            pltpu.VMEM((2, micro, length, width), BF16),
            pltpu.VMEM((width, rows), BF16),
            pltpu.VMEM((rows, width), BF16),
            square,
            square,
            square,
            pltpu.SemaphoreType.DMA((FETCHED,)),
            pltpu.SemaphoreType.DMA((len(BACK_PLAN), 7)),
            pltpu.SemaphoreType.DMA((len(BACK_PLAN), 7)),
            pltpu.SemaphoreType.DMA((UNITS, 2)),
            pltpu.SemaphoreType.DMA((UNITS, 2)),
            pltpu.SemaphoreType.DMA((4,)),
        ],
        compiler_params=pltpu.CompilerParams(
            collective_id=2, has_side_effects=True, vmem_limit_bytes=VMEM_LIMIT
        ),
        name="backward_attention",
    )(*terms, q, k, v, o, g, lse, tokens, wq, wk, wv, first)
    return outs[:9], outs[9]


def hand_out_kernel(*refs):
    (win, wout, wo, small) = refs[:4]
    qkv, small2, outs = refs[4:8], refs[8], refs[9:]
    (wq_o, qb, wk_o, wv_o, vb, wo_o, ob, g1, s1, win_o, ib, wout_o, outb, g2, s2) = outs
    win_o[...] = win[...]
    wout_o[...] = wout[...]
    wo_o[...] = wo[...]
    first = 0
    for group in qkv:
        lanes = group.shape[1] // 3
        for n, target in enumerate((wq_o, wk_o, wv_o)):
            target[:, first : first + lanes] = group[:, n * lanes : (n + 1) * lanes]
        first += lanes
    piece = qb.shape[1]
    qb[...] = small2[0:1, :piece]
    vb[...] = small2[1:2, :piece]
    for row, target in zip(range(2, 8), (ob, g1, s1, outb, g2, s2)):
        target[...] = small[row : row + 1, :piece]
    ib[...] = small[8:9, : ib.shape[1]]


def hand_out(win, wout, wo, small, qkv, small2, piece, wide):
    vmem_spec = pl.BlockSpec(memory_space=pltpu.VMEM)
    line = jax.ShapeDtypeStruct((1, piece), F32)
    like = lambda a: jax.ShapeDtypeStruct(a.shape, F32)
    shapes = [like(wo), line, like(wo), like(wo), line, like(wo), line, line, line, like(win)]
    shapes += [jax.ShapeDtypeStruct((1, wide), F32), like(wout), line, line, line]
    outs = pl.pallas_call(
        hand_out_kernel,
        in_specs=[vmem_spec] * 9,
        out_specs=[vmem_spec] * 15,
        out_shape=shapes,
        compiler_params=pltpu.CompilerParams(vmem_limit_bytes=VMEM_LIMIT),
        name="hand_out",
    )(win, wout, wo, small, *qkv, small2)
    return [a.reshape(-1) if a.shape[0] == 1 else a for a in outs]


def body(
    inputs,
    cotangent,
    query_weight,
    query_bias,
    key_weight,
    value_weight,
    value_bias,
    output_weight,
    output_bias,
    first_gain,
    first_shift,
    inner_weight,
    inner_bias,
    outer_weight,
    outer_bias,
    second_gain,
    second_shift,
):
    micro, _, length, width = inputs.shape
    devices = lax.axis_size(("seq", "grp"))
    piece, wide = query_bias.shape[0], inner_bias.shape[0]
    boxed = lax.axis_size("seq") == 2 and lax.axis_size("grp") == 16 and piece % 8 == 0
    own = inputs[:, 0]
    tokens = own.reshape(-1, width)
    upstream = cotangent[:, 0].reshape(-1, width)
    vectors = jnp.stack(
        (
            query_bias,
            value_bias,
            output_bias,
            first_gain,
            first_shift,
            outer_bias,
            second_gain,
            second_shift,
        )
    )
    vectors = jnp.pad(vectors, ((0, 8), (0, LANES - piece)))
    small = vectors + jnp.pad(inner_bias[None], ((8, 7), (0, LANES - wide)))
    shards = (
        small,
        query_weight,
        key_weight,
        value_weight,
        output_weight,
        inner_weight,
        outer_weight,
    )
    if boxed:
        fulls, made = forward_box(shards, own)
        small, wq, wk, wv, wo, win, wout = fulls
        queries, keys, values, attended, lse = made
    else:
        fulls = [lax.all_gather(a, ("seq", "grp"), axis=0, tiled=True) for a in shards]
        small, wq, wk, wv, wo, win, wout = fulls
        small = small.reshape(devices, 16, LANES)
        all_rows = lax.all_gather(own, "seq", axis=0)
        queries, keys, values = project(own, all_rows, wq, wk, wv, small)
        attended, lse = attend(queries, keys, values)
    flat = attended.reshape(-1, width)
    (
        layer_out,
        hidden_low,
        active,
        inner_grad,
        feed_grad,
        branch_grad,
        mixed_grad,
        first_grad,
        small_grad,
    ) = row_stage(tokens, flat, upstream, wo, win, wout, small)
    mixed_grad = mixed_grad.reshape(micro, length, width)
    win_grad = product(hidden_low, inner_grad, 768, 768)
    wout_grad = product(active, feed_grad, 768, 768)
    wo_grad = product(flat, branch_grad, 768, 768)
    if boxed:
        summed, input_grad = backward_box(
            win_grad,
            wout_grad,
            wo_grad,
            small_grad,
            queries,
            keys,
            values,
            attended,
            mixed_grad,
            lse,
            tokens,
            wq,
            wk,
            wv,
            first_grad,
        )
    else:
        dq, dk, dv = attend_back(queries, keys, values, attended, mixed_grad, lse)
        dk = lax.psum_scatter(dk, "seq", scatter_dimension=0)
        dv = lax.psum_scatter(dv, "seq", scatter_dimension=0)
        dq, dk, dv = (a.reshape(-1, width) for a in (dq, dk, dv))
        input_grad, small2_grad = input_stage(
            first_grad, dq, dk, dv, wq, wk, wv, (devices, 16, LANES)
        )
        groups = [
            jnp.concatenate([a[:, c : c + w] for a in (dq, dk, dv)], axis=1)
            for c, w in ((0, GROUP), (GROUP, GROUP), (2 * GROUP, PAIR), (2 * GROUP + PAIR, PAIR))
        ]
        terms = [win_grad, wout_grad, wo_grad, small_grad.reshape(-1, LANES)]
        terms += [product(tokens, a, 768, a.shape[1]) for a in groups]
        terms.append(small2_grad.reshape(-1, LANES))
        summed = [
            lax.psum_scatter(a.astype(F32), ("seq", "grp"), scatter_dimension=0, tiled=True)
            for a in terms
        ]
        summed = lax.optimization_barrier(summed)
    grads = hand_out(*summed[:4], summed[4:8], summed[8], piece, wide)
    return (layer_out.reshape(inputs.shape), input_grad.reshape(inputs.shape)) + tuple(grads)


def solution(mesh):
    rows = P(("seq", "grp"), None)
    line = P(("seq", "grp"))
    tokens = P(None, "grp", "seq", None)
    return jax.shard_map(
        body,
        mesh=mesh,
        in_specs=(
            tokens,
            tokens,
            rows,
            line,
            rows,
            rows,
            line,
            rows,
            line,
            line,
            line,
            rows,
            line,
            rows,
            line,
            line,
            line,
        ),
        out_specs=(
            tokens,
            tokens,
            rows,
            line,
            rows,
            rows,
            line,
            rows,
            line,
            line,
            line,
            rows,
            line,
            rows,
            line,
            line,
            line,
        ),
        check_vma=False,
    )
```

profile of v0, /device:TPU:0, one launch (start us, length us, event | category | flops | bytes accessed | tf_op | source)
XLA Modules:
  0.0 237.7 jit_solution(6718839295286433968)
XLA Ops:
  0.7 0.8 stack.35
  1.5 1.3 pad_add_fusion.refs_0_
  2.7 85.1 %forward_attention.1 = (bf16[2,4,2,2,16,128]{5,4,3,2,1,0:T(8,128)(2,1)}, bf16[2,4,2,2,24,768]{5,4,3,2,1,0:T(8,128)(2,1)}, bf16[2,4,2,2,24,768]{5,4,3,2,1,0:T(8,1...) custom-call(bf16[16,128]{1,0:T(8,128)(2,1)} %pad_add_fusion.refs_0_,, ...), custom_call_target="tpu_custom_call" | custom-call | tf_op jit(solution)/shard_map/forward_attention/pallas_call | solution.py:605
  87.9 41.3 %row_stage.1 = (bf16[1024,768]{1,0:T(8,128)(2,1)}, bf16[1024,768]{1,0:T(8,128)(2,1)}, bf16[1024,3072]{1,0:T(8,128)(2,1)}, bf16[1024,3072]{1,0:T(8,128)(2,1)}, bf...) custom-call(bf16[1024,768]{1,0:T(8,128)(2,1)} %bitcast.45, ...), custom_call_target="tpu_custom_call" | custom-call | tf_op jit(solution)/shard_map/row_stage/pallas_call | solution.py:748
  129.1 4.3 %weight_gradient.5 = bf16[768,768]{1,0:T(8,128)(2,1)} custom-call(bf16[1024,768]{1,0:T(8,128)(2,1)} %bitcast.43, bf16[1024,768]{1,0:T(8,128)(2,1)} %get-tuple-element.73.right_ref), custom_call_target="tpu_custom_call" | custom-call | tf_op jit(solution)/shard_map/weight_gradient/pallas_call | solution.py:793
  133.5 9.2 %weight_gradient.3 = bf16[768,3072]{1,0:T(8,128)(2,1)} custom-call(bf16[1024,768]{1,0:T(8,128)(2,1)} %get-tuple-element.69.left_ref, bf16[1024,3072]{1,0:T(8,128)(2,1)} %get-tuple-element.70.right_ref), custom_call_target="tpu_custom_call" | custom-call | tf_op jit(solution)/shard_map/weight_gradient/pallas_call | solution.py:793
  142.7 9.2 %weight_gradient.4 = bf16[3072,768]{1,0:T(8,128)(2,1)} custom-call(bf16[1024,3072]{1,0:T(8,128)(2,1)} %get-tuple-element.71.left_ref, bf16[1024,768]{1,0:T(8,128)(2,1)} %get-tuple-element.72.right_ref), custom_call_target="tpu_custom_call" | custom-call | tf_op jit(solution)/shard_map/weight_gradient/pallas_call | solution.py:793
  151.9 80.9 %backward_attention.1 = (f32[24,3072]{1,0:T(8,128)}, f32[96,768]{1,0:T(8,128)}, f32[24,768]{1,0:T(8,128)}, f32[16,128]{1,0:T(8,128)}, f32[24,768]{1,0:T(8,128)},...) custom-call(bf16[2,4,2,2,24,3072]{5,4,3,2,1,0:T(8,128)(2,1)} %bitcas, ...), custom_call_target="tpu_custom_call" | custom-call | tf_op jit(solution)/shard_map/backward_attention/pallas_call | solution.py:1037
  232.9 2.1 hand_out.1
  235.0 2.7 %copy.37 = bf16[2,1,512,768]{3,2,1,0:T(8,128)(2,1)} copy(bf16[2,1,512,768]{3,2,1,0:T(8,128)(2,1)} %bitcast.52) | data formatting | bytes 3145728
where the time goes:
time: 238 us
  Pallas kernels  232 us (97%)
  local copies, waits for them, and re-layouts  3.45 us (1%)
    pallas_call x1, Pallas kernels, forward_box(): pl.pallas_call(functools.partial(forward_kernel, chunks), out_shape=[jax....  85.1 us
    pallas_call x1, Pallas kernels, backward_box(): pl.pallas_call(functools.partial(backward_kernel, sizes), grid=(BACK_STEP...  80.9 us
    pallas_call x1, Pallas kernels, row_stage(): pl.pallas_call(rows_kernel, grid=(rows // block,), in_specs=[narrow] * 3...  41.3 us
    pallas_call x3, Pallas kernels, product(): pl.pallas_call(product_kernel, grid=(rows // block_m, cols // block_n), i...  22.8 us

commit v1 on v0

--- a/solution.py
+++ b/solution.py
@@ -559,11 +559,11 @@
             copy.start()
 
         def one(j, unused):
-            for n in range(3):
+            for n in range(4):
 
                 @pl.when(j == n)
                 def _():
-                    gather.step(ready + 3 * g + n)
+                    gather.step(ready + 4 * g + n)
 
             if g + 1 < groups:
 
@@ -583,7 +583,7 @@
 
         lax.fori_loop(0, 4, one, 0)
 
-    for n in range(ready + 3 * groups, gather.steps()):
+    for n in range(ready + 4 * groups, gather.steps()):
         gather.step(n)
     for i in range(3 * groups + 1, len(chunks)):
         gather.across(i).wait_recv()
@@ -649,9 +649,9 @@
     att_ref,
     cot_ref,
     wo_ref,
-    win_ref,
-    wout_ref,
     small_ref,
+    win_in,
+    wout_in,
     out_ref,
     hidden_ref,
     active_ref,
@@ -666,12 +666,19 @@
     slope,
     vecg,
     ibg,
+    win_ref,
+    wout_ref,
+    load,
 ):
     step = pl.program_id(0)
     chunks = win_ref.shape[1] // CHUNK
+    win_copy = pltpu.make_async_copy(win_in, win_ref, load.at[0])
+    wout_copy = pltpu.make_async_copy(wout_in, wout_ref, load.at[1])
 
     @pl.when(step == 0)
     def _():
+        win_copy.start()
+        wout_copy.start()
         vec[...] = spread(small_ref[:, 0:8].astype(F32), vec.shape[1])
         ib[...] = spread(small_ref[:, 8:16].astype(F32), ib.shape[1])
         vecg[...] = jnp.zeros_like(vecg)
@@ -685,6 +692,12 @@
     hidden = n1 * g1 + s1
     hidden_low = hidden.astype(BF16)
     hidden_ref[...] = hidden_low
+
+    @pl.when(step == 0)
+    def _():
+        win_copy.wait()
+        wout_copy.wait()
+
     total = hidden + outer_b
     for c in range(chunks):
         cols = slice(c * CHUNK, (c + 1) * CHUNK)
@@ -748,7 +761,9 @@
     return pl.pallas_call(
         rows_kernel,
         grid=(rows // block,),
-        in_specs=[narrow] * 3 + [whole(a) for a in (wo, win, wout, small)],
+        in_specs=[narrow] * 3
+        + [whole(wo), whole(small)]
+        + [pl.BlockSpec(memory_space=pl.ANY)] * 2,
         out_specs=[
             narrow,
             narrow,
@@ -777,10 +792,13 @@
             pltpu.VMEM((block, hidden_width), F32),
             pltpu.VMEM((8, width), F32),
             pltpu.VMEM((8, hidden_width), F32),
+            pltpu.VMEM(win.shape, BF16),
+            pltpu.VMEM(wout.shape, BF16),
+            pltpu.SemaphoreType.DMA((2,)),
         ],
         compiler_params=pltpu.CompilerParams(vmem_limit_bytes=VMEM_LIMIT),
         name="row_stage",
-    )(x, attended, cotangent, wo, win, wout, small)
+    )(x, attended, cotangent, wo, small, win, wout)
 
 
 def product_kernel(left_ref, right_ref, out_ref):
@@ -802,6 +820,72 @@
         compiler_params=pltpu.CompilerParams(vmem_limit_bytes=VMEM_LIMIT),
         name="weight_gradient",
     )(left, right)
+
+
+def products_kernel(hidden, inner, active, feed_in, flat_in, branch_in, win, wo, wout, *scratch):
+    feed, flat, branch, load = scratch
+    step = pl.program_id(0)
+    wide = pl.num_programs(0) // 2
+    copies = [
+        pltpu.make_async_copy(source, target, load.at[n])
+        for n, (source, target) in enumerate(
+            ((feed_in, feed), (flat_in, flat), (branch_in, branch))
+        )
+    ]
+
+    @pl.when(step == 0)
+    def _():
+        for copy in copies:
+            copy.start()
+
+    @pl.when(step < wide)
+    def _():
+        win[...] = dot_tn(hidden[...], inner[...]).astype(BF16)
+
+    @pl.when(step == wide - 1)
+    def _():
+        for copy in copies:
+            copy.wait()
+
+    @pl.when((step >= wide) & (step < 2 * wide))
+    def _():
+        wout[...] = dot_tn(active[...], feed[...]).astype(BF16)
+
+    @pl.when(step == 2 * wide)
+    def _():
+        wo[...] = dot_tn(flat[...], branch[...]).astype(BF16)
+
+
+def products(hidden, inner, active, feed, flat, branch):
+    tokens, width = hidden.shape
+    wide = inner.shape[1] // CHUNK
+    low = lambda *shape: jax.ShapeDtypeStruct(shape, BF16)
+    any_spec = pl.BlockSpec(memory_space=pl.ANY)
+    return pl.pallas_call(
+        products_kernel,
+        grid=(2 * wide + 1,),
+        in_specs=[
+            pl.BlockSpec((tokens, width), lambda i: (0, 0), pipeline_mode=pl.Buffered(1)),
+            pl.BlockSpec((tokens, CHUNK), lambda i: (0, jnp.clip(i, 0, wide - 1))),
+            pl.BlockSpec((tokens, CHUNK), lambda i: (0, jnp.clip(i - wide, 0, wide - 1))),
+            any_spec,
+            any_spec,
+            any_spec,
+        ],
+        out_specs=[
+            pl.BlockSpec((width, CHUNK), lambda i: (0, jnp.clip(i, 0, wide - 1))),
+            pl.BlockSpec((width, width), lambda i: (0, 0)),
+            pl.BlockSpec((CHUNK, width), lambda i: (jnp.clip(i - wide, 0, wide - 1), 0)),
+        ],
+        out_shape=[
+            low(width, inner.shape[1]),
+            low(width, width),
+            low(active.shape[1], width),
+        ],
+        scratch_shapes=[pltpu.VMEM((tokens, width), BF16)] * 3 + [pltpu.SemaphoreType.DMA((3,))],
+        compiler_params=pltpu.CompilerParams(vmem_limit_bytes=VMEM_LIMIT),
+        name="weight_gradients",
+    )(hidden, inner, active, feed, flat, branch)
 
 
 def input_kernel(first_ref, dq_ref, dk_ref, dv_ref, wq_ref, wk_ref, wv_ref, out_ref, vecg_ref, acc):
@@ -1186,9 +1270,9 @@
         small_grad,
     ) = row_stage(tokens, flat, upstream, wo, win, wout, small)
     mixed_grad = mixed_grad.reshape(micro, length, width)
-    win_grad = product(hidden_low, inner_grad, 768, 768)
-    wout_grad = product(active, feed_grad, 768, 768)
-    wo_grad = product(flat, branch_grad, 768, 768)
+    win_grad, wo_grad, wout_grad = products(
+        hidden_low, inner_grad, active, feed_grad, flat, branch_grad
+    )
     if boxed:
         summed, input_grad = backward_box(
             win_grad,

time: 238 us -> 230 us (0.966)
  Pallas kernels: 232 us -> 224 us
    pallas_call x1, Pallas kernels: 85.1 us -> 81 us  [forward_box(): pl.pallas_call(functools.partial(forward_kernel, chunks), out_shape=[jax....]
    pallas_call x3 -> x1, Pallas kernels: 22.8 us -> 18.9 us  [products(): pl.pallas_call(products_kernel, grid=(2 * wide + 1,), in_specs=[pl.BlockS...]
where the time goes in v1:
time: 230 us
  Pallas kernels  224 us (97%)
  local copies, waits for them, and re-layouts  3.45 us (2%)
    pallas_call x1, Pallas kernels, forward_box(): pl.pallas_call(functools.partial(forward_kernel, chunks), out_shape=[jax....  81 us
    pallas_call x1, Pallas kernels, backward_box(): pl.pallas_call(functools.partial(backward_kernel, sizes), grid=(BACK_STEP...  81 us
    pallas_call x1, Pallas kernels, row_stage(): pl.pallas_call(rows_kernel, grid=(rows // block,), in_specs=[narrow] * 3...  41.2 us
    pallas_call x1, Pallas kernels, products(): pl.pallas_call(products_kernel, grid=(2 * wide + 1,), in_specs=[pl.BlockS...  18.9 us

profile of v1, /device:TPU:0, one launch (start us, length us, event | category | flops | bytes accessed | tf_op | source)
XLA Modules:
  0.0 229.6 jit_solution(15052600466120985571)
XLA Ops:
  0.7 0.8 stack.35
  1.5 1.3 pad_add_fusion.refs_0_
  2.7 81.0 %forward_attention.1 = (bf16[2,4,2,2,16,128]{5,4,3,2,1,0:T(8,128)(2,1)}, bf16[2,4,2,2,24,768]{5,4,3,2,1,0:T(8,128)(2,1)}, bf16[2,4,2,2,24,768]{5,4,3,2,1,0:T(8,1...) custom-call(bf16[16,128]{1,0:T(8,128)(2,1)} %pad_add_fusion.refs_0_,, ...), custom_call_target="tpu_custom_call" | custom-call | tf_op jit(solution)/shard_map/forward_attention/pallas_call | solution.py:605
  83.7 41.2 %row_stage.1 = (bf16[1024,768]{1,0:T(8,128)(2,1)}, bf16[1024,768]{1,0:T(8,128)(2,1)}, bf16[1024,3072]{1,0:T(8,128)(2,1)}, bf16[1024,3072]{1,0:T(8,128)(2,1)}, bf...) custom-call(bf16[1024,768]{1,0:T(8,128)(2,1)} %bitcast.43, ...), custom_call_target="tpu_custom_call" | custom-call | tf_op jit(solution)/shard_map/row_stage/pallas_call | solution.py:761
  124.9 18.9 %weight_gradients.1 = (bf16[768,3072]{1,0:T(8,128)(2,1)}, bf16[768,768]{1,0:T(8,128)(2,1)}, bf16[3072,768]{1,0:T(8,128)(2,1)}) custom-call(bf16[1024,768]{1,0:T(8,128)(2,1)} %get-tuple-element.72.hidden, bf16[1024,3072]{1,0:T(8,128)(2,1)} %get-tuple-element.73.inner, bf16[1024,3072]{1,0:T(8,128)(2,1)} %get-tuple-element.74.active, ...), custom_call_target="tpu_custom_call" | custom-call | tf_op jit(solution)/shard_map/weight_gradients/pallas_call | solution.py:864
  143.8 81.0 %backward_attention.1 = (f32[24,3072]{1,0:T(8,128)}, f32[96,768]{1,0:T(8,128)}, f32[24,768]{1,0:T(8,128)}, f32[16,128]{1,0:T(8,128)}, f32[24,768]{1,0:T(8,128)},...) custom-call(bf16[2,4,2,2,24,3072]{5,4,3,2,1,0:T(8,128)(2,1)} %bitcas, ...), custom_call_target="tpu_custom_call" | custom-call | tf_op jit(solution)/shard_map/backward_attention/pallas_call | solution.py:1121
  224.8 2.1 hand_out.1
  226.9 2.7 %copy.37 = bf16[2,1,512,768]{3,2,1,0:T(8,128)(2,1)} copy(bf16[2,1,512,768]{3,2,1,0:T(8,128)(2,1)} %bitcast.51) | data formatting | bytes 3145728

commit v2 on v1

--- a/solution.py
+++ b/solution.py
@@ -206,7 +206,7 @@
         s = self.where[0]
         every = (slice(None),) * 3
         return pltpu.make_async_copy(
-            self.cut(self.terms, i, s, *every), self.cut(self.held, i, *every), self.load.at[i]
+            self.terms[i](s, *every), self.cut(self.held, i, *every), self.load.at[i]
         )
 
     def fetched(self, i):
@@ -216,7 +216,7 @@
         s, z, y, x = self.where
         every = (slice(None),) * 3
         return remote(
-            self.cut(self.terms, i, 1 - s, *every),
+            self.terms[i](1 - s, *every),
             self.cut(self.gots[0], i, *every),
             self.send.at[i, 0],
             self.recv.at[i, 0],
@@ -268,16 +268,12 @@
             if self.fetched(i):
                 self.fetch(i).start()
         elif t == 1:
-            if self.fetched(i):
+            if self.fetched(i) and i >= STAGED:
                 self.fetch(i).wait()
             self.across(i).wait_recv()
 
-            def add1(n, unused):
-                at = (n // 4, (n // 2) % 2, n % 2)
-                self.add(self.cut(self.held, i, *at), self.cut(self.gots[0], i, *at))
-                return unused
-
-            lax.fori_loop(0, 16, add1, 0)
+            every = (slice(None),) * 3
+            self.add(self.cut(self.held, i, *every), self.cut(self.gots[0], i, *every))
             for j in (0, 1):
                 self.first(i, j).start()
         elif t == 2:
@@ -291,7 +287,7 @@
                 self.add(self.cut(self.held, i, zz, yy, xx), self.cut(self.gots[1], i, zz, j))
                 return unused
 
-            lax.fori_loop(0, 8, add2, 0)
+            lax.fori_loop(0, 8, add2, 0, unroll=True)
             self.second(i).start()
         elif t == 3:
             self.second(i).wait_recv()
@@ -300,7 +296,7 @@
                 self.add(self.cut(self.held, i, zz, y, x), self.cut(self.gots[2], i, zz))
                 return unused
 
-            lax.fori_loop(0, 4, add3, 0)
+            lax.fori_loop(0, 4, add3, 0, unroll=True)
             for k in (1, 2, 3):
                 self.along_z(i, k).start()
         elif t == 4:
@@ -311,9 +307,14 @@
                 total = total + self.cut(self.gots[3], i, k)[...].astype(F32)
             self.out(i)[...] = total
 
+    def release(self, i):
+        self.fetch(i).wait()
+        self.across(i).wait_send()
+
     def sent(self):
         for i in range(len(self.chunks)):
-            self.across(i).wait_send()
+            if i >= STAGED:
+                self.across(i).wait_send()
             for j in (0, 1):
                 self.first(i, j).wait_send()
             self.second(i).wait_send()
@@ -340,8 +341,8 @@
 def attend_pair(queries, keys, values):
     length = queries.shape[0]
     mixed, logs = [], []
-    for head in (0, 1):
-        scores = dot_nt(pick(queries, head), keys)
+    both = [dot_nt(pick(queries, head), keys) for head in (0, 1)]
+    for head, scores in enumerate(both):
         top = jnp.max(scores, axis=1, keepdims=True)
         powers = jnp.exp(scores - top)
         total = jnp.sum(powers, axis=1, keepdims=True)
@@ -358,13 +359,14 @@
     dk = jnp.zeros(keys.shape, F32)
     dv = jnp.zeros(keys.shape, F32)
     dq_t = []
+    both = []
     for head in (0, 1):
-        offset = jnp.sum(products[64 * head : 64 * head + 64], axis=0, keepdims=True)
         q_head = pick(queries, head)
         g_head = pick(grad, head)
-        scores_t = dot_nt(keys, q_head)
+        both.append((q_head, g_head, dot_nt(keys, q_head), dot_nt(values, g_head)))
+    for head, (q_head, g_head, scores_t, slopes_t) in enumerate(both):
+        offset = jnp.sum(products[64 * head : 64 * head + 64], axis=0, keepdims=True)
         probs_t = jnp.exp(scores_t - logs[head : head + 1, :])
-        slopes_t = dot_nt(values, g_head)
         score_grad_t = (probs_t * (slopes_t - offset)).astype(BF16)
         dv += dot_nn(probs_t.astype(BF16), g_head)
         dk += dot_nn(score_grad_t, q_head)
@@ -699,16 +701,20 @@
         wout_copy.wait()
 
     total = hidden + outer_b
+    ahead = dot_nn(hidden_low, win_ref[:, :CHUNK])
     for c in range(chunks):
         cols = slice(c * CHUNK, (c + 1) * CHUNK)
-        v = dot_nn(hidden_low, win_ref[:, cols]) + ib[0:1, cols]
+        v = ahead + ib[0:1, cols]
+        if c + 1 < chunks:
+            ahead = dot_nn(hidden_low, win_ref[:, (c + 1) * CHUNK : (c + 2) * CHUNK])
         square = v * v
         t = jnp.tanh(v * (GELU_C + (GELU_C * GELU_A) * square))
         half = 0.5 * (1.0 + t)
-        active = (v * half).astype(BF16)
+        gated = v * half
+        active = gated.astype(BF16)
         active_ref[:, cols] = active
-        slope[:, cols] = half + (0.5 * v) * (1.0 - t * t) * (
-            GELU_C + (3.0 * GELU_C * GELU_A) * square
+        slope[:, cols] = half + gated * (1.0 - half) * (
+            (2.0 * GELU_C) + (6.0 * GELU_C * GELU_A) * square
         )
         total = total + dot_nn(active, wout_ref[cols, :])
     centred = total - mean_rows(total)
@@ -724,9 +730,12 @@
     vecg[7:8] += jnp.sum(e, axis=0, keepdims=True)
     vecg[5:6] += jnp.sum(feed.astype(F32), axis=0, keepdims=True)
     e = second
+    ahead = dot_nt(feed, wout_ref[:CHUNK, :])
     for c in range(chunks):
         cols = slice(c * CHUNK, (c + 1) * CHUNK)
-        inner_grad = (dot_nt(feed, wout_ref[cols, :]) * slope[:, cols]).astype(BF16)
+        inner_grad = (ahead * slope[:, cols]).astype(BF16)
+        if c + 1 < chunks:
+            ahead = dot_nt(feed, wout_ref[(c + 1) * CHUNK : (c + 2) * CHUNK, :])
         inner_grad_ref[:, cols] = inner_grad
         ibg[0:1, cols] += jnp.sum(inner_grad.astype(F32), axis=0, keepdims=True)
         e = e + dot_nt(inner_grad, win_ref[:, cols])
@@ -930,49 +939,58 @@
     )(first, dq, dk, dv, wq, wk, wv)
 
 
-PLAN_IN = ((1, 2, 6, 9, 11), (1, 4, 6, 8, 18), (1, 2, 5, 7, 19), (0, 1, 9, 11, 16),)
-PLAN_OUT = ((0, 1, 5, 9, 19), (9, 10, 13, 15, 17), (2, 8, 11, 13, 19))
-PLAN_O, PLAN_SMALL, PLAN_SMALL2 = (2, 5, 9, 10, 19), (5, 6, 9, 10, 19), (13, 15, 16, 18, 24)
+PLAN_IN = ((1, 2, 5, 8, 11), (2, 3, 7, 10, 14), (3, 5, 9, 12, 15), (4, 7, 11, 13, 16),)
+PLAN_OUT = ((9, 10, 13, 16, 19), (10, 12, 15, 17, 20), (12, 14, 17, 19, 22))
+PLAN_O, PLAN_SMALL, PLAN_SMALL2 = (5, 9, 12, 15, 18), (5, 9, 12, 15, 18), (22, 23, 25, 27, 30)
 PLAN_QKV = (
-    (6, 7, 10, 12, 19),
-    (10, 11, 14, 16, 23),
-    (13, 14, 16, 20, 23),
-    (13, 15, 20, 21, 24),
+    (15, 16, 19, 21, 24),
+    (19, 20, 22, 24, 27),
+    (21, 22, 24, 26, 29),
+    (22, 23, 25, 27, 30),
 )
 G_IN, G_OUT, G_O, G_SMALL, G_QKV, G_SMALL2 = 0, 1, 2, 3, 4, 8
 UNITS = 12
-BACK_STEPS = UNITS + 5
+FIRST = 9
+STAGED = 5
+BACK_STEPS = FIRST + UNITS + 5
 BACK_PLAN = (
-    [(G_OUT, c * GROUP, GROUP, plan) for c, plan in enumerate(PLAN_OUT)]
-    + [(G_IN, c * CHUNK, CHUNK, plan) for c, plan in enumerate(PLAN_IN)]
+    [(G_IN, c * CHUNK, CHUNK, plan) for c, plan in enumerate(PLAN_IN)]
     + [(G_O, 0, CHUNK, PLAN_O), (G_SMALL, 0, LANES, PLAN_SMALL)]
+    + [(G_OUT, c * GROUP, GROUP, plan) for c, plan in enumerate(PLAN_OUT)]
     + [(G_QKV + g, 0, 3 * w, plan) for g, (w, plan) in enumerate(zip((256, 256, 128, 128), PLAN_QKV))]
     + [(G_SMALL2, 0, LANES, PLAN_SMALL2)]
 )
-FETCHED = 9
+FETCHED = 6
 
 
 def unit_of(step):
-    u = jnp.clip(step, 0, UNITS - 1)
+    u = jnp.clip(step - FIRST, 0, UNITS - 1)
     return u % 2, u // 2
 
 
 def backward_kernel(sizes, *refs):
-    terms1 = refs[:4]
-    (q_ref, k_ref, v_ref, o_ref, g_ref, lse_ref, x_in, wq_in, wk_in, wv_in, first_ref) = refs[4:15]
-    outs, dx_ref = refs[15:24], refs[24]
-    held1 = refs[25:29]
-    broad, slim, small2, sums = refs[29:33]
-    gots = got_levels(refs[33:69], 9)
-    dq_all, dk_all, dv_all, away, far, x_t, x_v, wq_v, wk_v, wv_v = refs[69:79]
-    load, send, recv, far_send, far_recv, bring = refs[79:]
+    hidden_in, inner_in, active_in, feed_in, flat_in, branch_in, small_in = refs[:7]
+    (q_ref, k_ref, v_ref, o_ref, g_ref, lse_ref, x_in, wq_in, wk_in, wv_in, first_ref) = refs[7:18]
+    outs, dx_ref = refs[18:27], refs[27]
+    held1 = refs[28:32]
+    broad, slim, small2, sums = refs[32:36]
+    gots = got_levels(refs[36:72], 9)
+    dq_all, dk_all, dv_all, away, far, x_t, x_v, wq_v, wk_v, wv_v, out_far = refs[72:83]
+    load, send, recv, far_send, far_recv, bring, feed_sem = refs[83:]
     where = place()
     s, z, y, x = where
     step = pl.program_id(0)
     length = q_ref.shape[1]
     rows = dq_all.shape[0] * length
     chunks = [(a, 0, sizes[a][0], c, nc) for a, c, nc, _ in BACK_PLAN]
-    terms = list(terms1) + [a.at[g] for a in (broad, slim) for g in (0, 1)] + [small2]
+
+    def view(ref, cols=slice(None)):
+        return lambda *at: ref.at[(*at, slice(None), cols)]
+
+    terms = [view(broad.at[n % 2]) for n in range(STAGED)] + [view(small_in)]
+    for _, c, nc, _ in BACK_PLAN[6:9]:
+        terms.append(lambda s, *at, cols=slice(c, c + nc): out_far.at[(*at, slice(None), cols)])
+    terms += [view(a.at[g]) for a in (broad, slim) for g in (0, 1)] + [view(small2)]
     held = list(held1) + [a.at[g, s] for a in (broad, slim) for g in (0, 1)] + [small2.at[s]]
     scatter = Scatter(terms, held, gots, outs, load, send, recv, chunks, where)
     copies = [
@@ -980,8 +998,20 @@
         for n, (a, b) in enumerate(zip((x_in, wq_in, wk_in, wv_in), (x_v, wq_v, wk_v, wv_v)))
     ]
 
+    operands = [
+        pltpu.make_async_copy(a, b, feed_sem.at[n])
+        for n, (a, b) in enumerate(
+            ((hidden_in, dk_all), (feed_in, dv_all), (branch_in, dq_all), (flat_in, x_v))
+        )
+    ]
+
+    def operand(n):
+        source = inner_in if n < 4 else active_in
+        cols = slice((n % 4) * CHUNK, (n % 4 + 1) * CHUNK)
+        return pltpu.make_async_copy(source.at[:, :, cols], far.at[n % 2], feed_sem.at[4 + n % 2])
+
     def far_copies(u):
-        m, p = unit_of(u)
+        m, p = unit_of(u + FIRST)
         lanes = pl.ds(pl.multiple_of(p * PAIR, PAIR), PAIR)
         target = device(1 - s, z, y, x)
         return [
@@ -993,30 +1023,80 @@
 
     @pl.when(step == 0)
     def _():
-        for copy in copies:
+        operands[0].start()
+        operand(0).start()
+        operand(1).start()
+        for copy in operands[1:] + copies[1:]:
             copy.start()
         greet(s, z, y, x)
 
     for n in range(BACK_STEPS):
         todo = [(t, i) for i, c in enumerate(BACK_PLAN) for t, at in enumerate(c[3]) if at == n]
-        if todo:
+        if todo or 2 <= n < 2 + STAGED:
 
             @pl.when(step == n)
             def _():
+                if 2 <= n < 2 + STAGED:
+                    scatter.release(n - 2)
                 for t, i in sorted(todo, reverse=True):
                     scatter.stage(t, i)
 
-    @pl.when((step > 0) & (step < UNITS))
-    def _():
-        for copy in far_copies(step - 1):
+    whole = lambda ref: ref[...].reshape(rows, CHUNK)
+    for n in range(FIRST):
+
+        @pl.when(step == n)
+        def _():
+            for at, which in ((0, 0), (4, 2), (4, 3), (5, 1)):
+                if n == at:
+                    operands[which].wait()
+            if n != 4:
+                operand(n - n // 5).wait()
+
+    @pl.when(step < 4)
+    def _():
+        value = dot_tn(whole(dk_all), whole(far.at[step % 2])).astype(BF16)
+        broad[step % 2] = value.reshape((2, 4, 2, 2) + sizes[G_O])
+
+    @pl.when(step == 4)
+    def _():
+        value = dot_tn(x_v[...], whole(dq_all)).astype(BF16)
+        broad[0] = value.reshape((2, 4, 2, 2) + sizes[G_O])
+        copies[0].start()
+
+    @pl.when((step > 4) & (step < FIRST))
+    def _():
+        c = step - 5
+        value = dot_tn(whole(far.at[c % 2]), whole(dv_all)).astype(BF16)
+        value = value.reshape((2, 2, 2) + sizes[G_OUT])
+        half = pl.ds((c % 2) * 2, 2)
+
+        @pl.when(s == c // 2)
+        def _():
+            held1[G_OUT][half] = value
+
+        @pl.when(s != c // 2)
+        def _():
+            out_far[half] = value
+
+    for n in range(FIRST):
+        k = n - n // 5
+        if n != 4 and k + 2 < 8:
+
+            @pl.when(step == n)
+            def _():
+                operand(k + 2).start()
+
+    @pl.when((step > FIRST) & (step < FIRST + UNITS))
+    def _():
+        for copy in far_copies(step - FIRST - 1):
             copy.start()
 
-    @pl.when(step == 1)
+    @pl.when(step == FIRST)
     def _():
         copies[0].wait()
         x_t[...] = jnp.transpose(x_v[...])
 
-    @pl.when(step < UNITS)
+    @pl.when((step >= FIRST) & (step < FIRST + UNITS))
     def _():
         m, p = unit_of(step)
         lanes = pl.ds(pl.multiple_of(p * PAIR, PAIR), PAIR)
@@ -1026,10 +1106,10 @@
         dq_all[m, :, lanes] = dq
         dk_all[m, :, lanes] = dk[:length]
         dv_all[m, :, lanes] = dv[:length]
-        away[step, 0] = dk[length:]
-        away[step, 1] = dv[length:]
-
-    @pl.when(step == UNITS)
+        away[step - FIRST, 0] = dk[length:]
+        away[step - FIRST, 1] = dv[length:]
+
+    @pl.when(step == FIRST + UNITS)
     def _():
         for copy in far_copies(UNITS - 1):
             copy.start()
@@ -1048,17 +1128,17 @@
                 (2, 4, 2, 2) + (sizes[G_QKV][0], lanes)
             )
 
-    @pl.when((step == 5) | (step == 9))
-    def _():
-        g = (step - 5) // 4
+    @pl.when((step == FIRST + 5) | (step == FIRST + 9))
+    def _():
+        g = (step - FIRST - 5) // 4
         products(broad, g, 4 * g, 4, g * GROUP, GROUP)
 
-    @pl.when((step == 11) | (step == 12))
-    def _():
-        g = step - 11
+    @pl.when((step == FIRST + 11) | (step == FIRST + 12))
+    def _():
+        g = step - FIRST - 11
         products(slim, g, 8 + 2 * g, 2, 2 * GROUP + g * PAIR, PAIR)
 
-    @pl.when(step == UNITS)
+    @pl.when(step == FIRST + UNITS)
     def _():
         sums[...] = jnp.zeros_like(sums)
         for n, whole in enumerate((dq_all, dv_all)):
@@ -1071,10 +1151,10 @@
         for copy in copies[1:]:
             copy.wait()
 
-    @pl.when(step > UNITS)
+    @pl.when(step > FIRST + UNITS)
     def _():
         block = first_ref.shape[0]
-        r = step - UNITS - 1
+        r = step - FIRST - UNITS - 1
         per = length // block
         at = pl.ds(pl.multiple_of((r % per) * block, block), block)
         dx_ref[...] = (
@@ -1096,16 +1176,17 @@
         scatter.sent()
 
 
-def backward_box(win_grad, wout_grad, wo_grad, small, q, k, v, o, g, lse, tokens, wq, wk, wv, first):
+def backward_box(
+    hidden, inner, active, feed, flat, branch, small, q, k, v, o, g, lse, tokens, wq, wk, wv, first
+):
     micro, length, width = q.shape
-    rows = tokens.shape[0]
+    rows, hidden_width = inner.shape
     narrow, thin = (width // 32, width), (16, LANES)
-    sizes = [(width // 32, win_grad.shape[1]), (wout_grad.shape[0] // 32, width), narrow, thin]
+    sizes = [(width // 32, hidden_width), (hidden_width // 32, width), narrow, thin]
     sizes += [(narrow[0], 3 * w) for w in (GROUP, GROUP, PAIR, PAIR)] + [thin]
-    terms = [
-        a.reshape((2, 4, 2, 2) + size)
-        for a, size in zip((win_grad, wout_grad, wo_grad, small), sizes)
-    ]
+    split = lambda a: a.reshape(micro, length, a.shape[1])
+    given = [split(hidden), split(inner), split(active), split(feed), flat, split(branch)]
+    given.append(small.reshape((2, 4, 2, 2) + thin))
     block = rows // 4
 
     def at(i):
@@ -1114,14 +1195,14 @@
     row = pl.BlockSpec((1, length, PAIR), lambda i: (at(i)[0], 0, at(i)[1]))
     col = pl.BlockSpec((2, 1, length, PAIR), lambda i: (0, at(i)[0], 0, at(i)[1]))
     log = pl.BlockSpec((1, 1, 2, length), lambda i: (at(i)[0], at(i)[1], 0, 0))
-    flat = pl.BlockSpec((block, width), lambda i: (jnp.clip(i - UNITS - 1, 0, 3), 0))
+    flat = pl.BlockSpec((block, width), lambda i: (jnp.clip(i - FIRST - UNITS - 1, 0, 3), 0))
     any_spec = pl.BlockSpec(memory_space=pl.ANY)
     square = pltpu.VMEM((width, width), BF16)
     low = pltpu.VMEM((micro, length, width), BF16)
     outs = pl.pallas_call(
         functools.partial(backward_kernel, sizes),
         grid=(BACK_STEPS,),
-        in_specs=[any_spec] * 4 + [row, col, col, row, row, log] + [any_spec] * 4 + [flat],
+        in_specs=[any_spec] * 7 + [row, col, col, row, row, log] + [any_spec] * 4 + [flat],
         out_specs=[pl.BlockSpec(size, lambda i: (0, 0)) for size in sizes] + [flat],
         out_shape=[jax.ShapeDtypeStruct(size, F32) for size in sizes]
         + [jax.ShapeDtypeStruct((rows, width), BF16)],
@@ -1144,24 +1225,27 @@
             square,
             square,
             square,
+            pltpu.VMEM((4, 2, 2) + sizes[G_OUT], BF16),
             pltpu.SemaphoreType.DMA((FETCHED,)),
             pltpu.SemaphoreType.DMA((len(BACK_PLAN), 7)),
             pltpu.SemaphoreType.DMA((len(BACK_PLAN), 7)),
             pltpu.SemaphoreType.DMA((UNITS, 2)),
             pltpu.SemaphoreType.DMA((UNITS, 2)),
             pltpu.SemaphoreType.DMA((4,)),
+            pltpu.SemaphoreType.DMA((6,)),
         ],
         compiler_params=pltpu.CompilerParams(
             collective_id=2, has_side_effects=True, vmem_limit_bytes=VMEM_LIMIT
         ),
         name="backward_attention",
-    )(*terms, q, k, v, o, g, lse, tokens, wq, wk, wv, first)
+    )(*given, q, k, v, o, g, lse, tokens, wq, wk, wv, first)
     return outs[:9], outs[9]
 
 
 def hand_out_kernel(*refs):
     (win, wout, wo, small) = refs[:4]
-    qkv, small2, outs = refs[4:8], refs[8], refs[9:]
+    qkv, small2, dx, dx_o, outs = refs[4:8], refs[8], refs[9], refs[10], refs[11:]
+    dx_o[...] = dx[...]
     (wq_o, qb, wk_o, wv_o, vb, wo_o, ob, g1, s1, win_o, ib, wout_o, outb, g2, s2) = outs
     win_o[...] = win[...]
     wout_o[...] = wout[...]
@@ -1180,7 +1264,7 @@
     ib[...] = small[8:9, : ib.shape[1]]
 
 
-def hand_out(win, wout, wo, small, qkv, small2, piece, wide):
+def hand_out(win, wout, wo, small, qkv, small2, dx, piece, wide):
     vmem_spec = pl.BlockSpec(memory_space=pltpu.VMEM)
     line = jax.ShapeDtypeStruct((1, piece), F32)
     like = lambda a: jax.ShapeDtypeStruct(a.shape, F32)
@@ -1188,13 +1272,13 @@
     shapes += [jax.ShapeDtypeStruct((1, wide), F32), like(wout), line, line, line]
     outs = pl.pallas_call(
         hand_out_kernel,
-        in_specs=[vmem_spec] * 9,
-        out_specs=[vmem_spec] * 15,
-        out_shape=shapes,
+        in_specs=[vmem_spec] * 10,
+        out_specs=[vmem_spec] * 16,
+        out_shape=[jax.ShapeDtypeStruct(dx.shape, dx.dtype)] + shapes,
         compiler_params=pltpu.CompilerParams(vmem_limit_bytes=VMEM_LIMIT),
         name="hand_out",
-    )(win, wout, wo, small, *qkv, small2)
-    return [a.reshape(-1) if a.shape[0] == 1 else a for a in outs]
+    )(win, wout, wo, small, *qkv, small2, dx)
+    return outs[0], [a.reshape(-1) if a.shape[0] == 1 else a for a in outs[1:]]
 
 
 def body(
@@ -1223,7 +1307,8 @@
     own = inputs[:, 0]
     tokens = own.reshape(-1, width)
     upstream = cotangent[:, 0].reshape(-1, width)
-    vectors = jnp.stack(
+    small = jnp.zeros((16, LANES), BF16)
+    for row, vector in enumerate(
         (
             query_bias,
             value_bias,
@@ -1233,10 +1318,10 @@
             outer_bias,
             second_gain,
             second_shift,
-        )
-    )
-    vectors = jnp.pad(vectors, ((0, 8), (0, LANES - piece)))
-    small = vectors + jnp.pad(inner_bias[None], ((8, 7), (0, LANES - wide)))
+            inner_bias,
+        )
+    ):
+        small += jnp.pad(vector[None], ((row, 15 - row), (0, LANES - vector.shape[0])))
     shards = (
         small,
         query_weight,
@@ -1270,14 +1355,14 @@
         small_grad,
     ) = row_stage(tokens, flat, upstream, wo, win, wout, small)
     mixed_grad = mixed_grad.reshape(micro, length, width)
-    win_grad, wo_grad, wout_grad = products(
-        hidden_low, inner_grad, active, feed_grad, flat, branch_grad
-    )
     if boxed:
         summed, input_grad = backward_box(
-            win_grad,
-            wout_grad,
-            wo_grad,
+            hidden_low,
+            inner_grad,
+            active,
+            feed_grad,
+            flat,
+            branch_grad,
             small_grad,
             queries,
             keys,
@@ -1292,6 +1377,9 @@
             first_grad,
         )
     else:
+        win_grad, wo_grad, wout_grad = products(
+            hidden_low, inner_grad, active, feed_grad, flat, branch_grad
+        )
         dq, dk, dv = attend_back(queries, keys, values, attended, mixed_grad, lse)
         dk = lax.psum_scatter(dk, "seq", scatter_dimension=0)
         dv = lax.psum_scatter(dv, "seq", scatter_dimension=0)
@@ -1311,7 +1399,7 @@
             for a in terms
         ]
         summed = lax.optimization_barrier(summed)
-    grads = hand_out(*summed[:4], summed[4:8], summed[8], piece, wide)
+    input_grad, grads = hand_out(*summed[:4], summed[4:8], summed[8], input_grad, piece, wide)
     return (layer_out.reshape(inputs.shape), input_grad.reshape(inputs.shape)) + tuple(grads)
 
 

time: 230 us -> 221 us (0.961)
  Pallas kernels: 224 us -> 218 us
  local copies, waits for them, and re-layouts: 3.45 us -> 0 us
    pallas_call x2 -> x1, Pallas kernels: 21 us -> 3.26 us  [hand_out(): pl.pallas_call(hand_out_kernel, in_specs=[vmem_spec] * 10, out_specs=[vme...]
    pallas_call x1, Pallas kernels: 81 us -> 92.9 us  [backward_box(): pl.pallas_call(functools.partial(backward_kernel, sizes), grid=(BACK_STEP...]
    unnamed x1 -> x0, local copies, waits for them, and re-layouts: 2.65 us -> none
where the time goes in v2:
time: 221 us
  Pallas kernels  218 us (99%)
    pallas_call x1, Pallas kernels, backward_box(): pl.pallas_call(functools.partial(backward_kernel, sizes), grid=(BACK_STEP...  92.9 us
    pallas_call x1, Pallas kernels, forward_box(): pl.pallas_call(functools.partial(forward_kernel, chunks), out_shape=[jax....  81 us
    pallas_call x1, Pallas kernels, row_stage(): pl.pallas_call(rows_kernel, grid=(rows // block,), in_specs=[narrow] * 3...  41 us

profile of v2, /device:TPU:0, one launch (start us, length us, event | category | flops | bytes accessed | tf_op | source)
XLA Modules:
  0.0 220.5 jit_solution(151513706145758195)
XLA Ops:
  0.7 1.4 pad_add_fusion.refs_0_
  2.1 81.0 %forward_attention.1 = (bf16[2,4,2,2,16,128]{5,4,3,2,1,0:T(8,128)(2,1)}, bf16[2,4,2,2,24,768]{5,4,3,2,1,0:T(8,128)(2,1)}, bf16[2,4,2,2,24,768]{5,4,3,2,1,0:T(8,1...) custom-call(bf16[16,128]{1,0:T(8,128)(2,1)} %pad_add_fusion.refs_0_,, ...), custom_call_target="tpu_custom_call" | custom-call | tf_op jit(solution)/shard_map/forward_attention/pallas_call | solution.py:607
  83.1 41.0 %row_stage.1 = (bf16[1024,768]{1,0:T(8,128)(2,1)}, bf16[1024,768]{1,0:T(8,128)(2,1)}, bf16[1024,3072]{1,0:T(8,128)(2,1)}, bf16[1024,3072]{1,0:T(8,128)(2,1)}, bf...) custom-call(bf16[1024,768]{1,0:T(8,128)(2,1)} %bitcast.45, ...), custom_call_target="tpu_custom_call" | custom-call | tf_op jit(solution)/shard_map/row_stage/pallas_call | solution.py:770
  124.1 92.9 %backward_attention.1 = (f32[24,3072]{1,0:T(8,128)}, f32[96,768]{1,0:T(8,128)}, f32[24,768]{1,0:T(8,128)}, f32[16,128]{1,0:T(8,128)}, f32[24,768]{1,0:T(8,128)},...) custom-call(bf16[2,512,768]{2,1,0:T(8,128)(2,1)} %bitcast.51, ...), custom_call_target="tpu_custom_call" | custom-call | tf_op jit(solution)/shard_map/backward_attention/pallas_call | solution.py:1202
  217.1 3.3 %hand_out.1 = (bf16[1024,768]{1,0:T(8,128)(2,1)}, f32[24,768]{1,0:T(8,128)}, f32[1,24]{1,0:T(1,128)}, f32[24,768]{1,0:T(8,128)}, f32[24,768]{1,0:T(8,128)}, /*in...) custom-call(f32[24,3072]{1,0:T(8,128)} %get-tuple-element.85.refs_0_, ...), custom_call_target="tpu_custom_call" | custom-call | tf_op jit(solution)/shard_map/hand_out/pallas_call | solution.py:1273
